TPU v7x, 32 devices: a whole 2x2x4 slice. The times are simulated.
32 devices in a mesh: group: 2 (over x), inp: 16 (over z, y, core).
Axes of the slice: x: 2, y: 2, z: 4, core: 2. Of those that a mesh axis runs over, the one named last changes fastest.
Arguments:
- raw: bfloat16 [4096, 268288], P(('group', 'inp')), parts along dimension 0, may hold values from -180 to 180
- pfb_taps: float32 [4, 2048], replicated, may hold values from -0.0625 to 0.0625
- flags: int32 [4096], P(('group', 'inp')), parts along dimension 0, may hold values 0 or 1
- chan_table: int32 [8], P('group'), parts along dimension 0, may hold values from 0 to 1023
Outputs:
- visibility: bfloat16 [16384, 2, 2048], P(('group', 'inp')), parts along dimension 0
There are 2 independent parts, one for each index of `group`. A program takes and returns all parts, laid end to end along the dimension named above; an argument that names none is the same for every part. Nothing has to cross between parts.
All inputs are finite; a program needn't handle non-finite values. No bound on the sum of `flags` on one device may be relied on, other than what follows from the above.
Results may differ from a plain program's by a relative error of at most 0.0074.
Values may be sent and summed in bfloat16 or wider, within the bound.
A program may use at most 256 MiB of HBM per device.

v0:
```python
import math

import jax
import jax.numpy as jnp
from jax import lax
from jax.sharding import PartitionSpec as P

FFT_LEN = 2048
FILTER_TAPS = 4
SPECTRA = 128
ROW_BLOCKS = 4


def make_basis(chan_table):
    sample_index = jnp.arange(FFT_LEN, dtype=jnp.int32)
    phase_steps = sample_index[:, None] * chan_table[None, :] % FFT_LEN
    angle = phase_steps.astype(jnp.float32) * (2.0 * math.pi / FFT_LEN)
    return jnp.concatenate([jnp.cos(angle), -jnp.sin(angle)], axis=1).astype(jnp.bfloat16)


def row_product(left, right):
    return lax.dot_general(
        left, right, (((1,), (1,)), ((), ())), preferred_element_type=jnp.float32
    )


def on_device(raw, pfb_taps, flags, chan_table):
    width = raw.shape[0]
    count = SPECTRA
    frames = raw.reshape(width, count + FILTER_TAPS - 1, FFT_LEN)
    filtered = pfb_taps[0] * frames[:, 0:count, :].astype(jnp.float32)
    for tap in range(1, FILTER_TAPS):
        filtered = filtered + pfb_taps[tap] * frames[:, tap : tap + count, :].astype(jnp.float32)
    filtered = filtered.astype(jnp.bfloat16).reshape(width * count, FFT_LEN)
    basis = make_basis(chan_table)
    selected = chan_table.shape[0]
    plain = jnp.dot(filtered, basis, preferred_element_type=jnp.float32)
    plain = plain.reshape(width, count, 2 * selected) * flags.astype(jnp.float32)[:, None, None]
    spectra = jnp.transpose(plain.astype(jnp.bfloat16), (0, 2, 1))
    grouped = spectra.reshape(width, 2, selected, count)
    squares = lax.dot_general(
        raw, raw, (((1,), (1,)), ((0,), (0,))), preferred_element_type=jnp.float32
    )
    power = squares * (1.0 / raw.shape[1]) + 1e-06
    power_all = lax.all_gather(power, "inp", axis=0, tiled=True)
    outgoing = jnp.repeat(grouped, ROW_BLOCKS, axis=2).reshape(
        width, 2, selected * ROW_BLOCKS * count
    )
    columns = lax.all_to_all(outgoing, "inp", split_axis=2, concat_axis=0, tiled=True)
    block_index = lax.axis_index("inp") % ROW_BLOCKS
    rows_here = columns.shape[0] // ROW_BLOCKS
    depth = columns.shape[2]
    mine = lax.dynamic_slice_in_dim(columns, block_index * rows_here, rows_here, 0)
    flat_columns = columns.reshape(columns.shape[0], 2 * depth)
    real_vis = row_product(mine.reshape(rows_here, 2 * depth), flat_columns)
    imag_vis = row_product(mine[:, 1, :], columns[:, 0, :]) - row_product(
        mine[:, 0, :], columns[:, 1, :]
    )
    scales = lax.rsqrt(power_all)
    my_scales = lax.dynamic_slice_in_dim(scales, block_index * rows_here, rows_here, 0)
    left_scale = my_scales[:, None] * (1.0 / SPECTRA)
    right_scale = scales[None, :]
    real_out = real_vis * left_scale * right_scale
    imag_out = imag_vis * left_scale * right_scale
    return jnp.stack([real_out, imag_out], axis=1).astype(jnp.bfloat16)


def solution(mesh):
    placed = (P(("group", "inp"), None), P(), P(("group", "inp")), P("group"))
    return jax.shard_map(
        on_device,
        mesh=mesh,
        in_specs=placed,
        out_specs=P(("group", "inp"), None, None),
        check_vma=False,
    )
```

profile of v0, /device:TPU:0, one launch (start us, length us, event | category | flops | bytes accessed | tf_op | source)
XLA Modules:
  0.0 240.5 jit_solution(4038197805007759036)
XLA Ops:
  0.0 0.0 copy-start
  0.0 0.0 copy-start.2
  0.0 0.0 copy-start.1
  0.0 88.5 %copy.17 = bf16[128,268288]{0,1:T(8,128)(2,1)} copy(bf16[128,268288]{1,0:T(8,128)(2,1)} %param.4) | data formatting | bytes 137363456 | tf_op args[0]
  88.5 0.0 copy-done
  88.5 0.0 copy-done.2
  88.5 0.0 copy-done.1
  88.5 0.4 cosine_convert_fusion
  88.9 83.6 %fusion.5 = bf16[128,128,8]{0,2,1:T(8,128)(2,1)S(1)} fusion(bf16[128,131,2048]{0,2,1:T(8,128)(2,1)} %bitcast.1, f32[2048]{0:T(1024)S(1)} %bitcast.59, f32[2048]{0:T(1024)S(1)} %bitcast.60, f32[2048]{0:T(1024)S(1)} %bitcast.58, f32[2048]{0:T(1024)S(1)} %bitcast.57, f32[128]{0:T(128)S(1)} %convert_element_type.36, bf16[2048,4]{0,1:T(4,128)(2,1)S(1)} %get-tuple-element.10, ...), kind=kOutput, calls=%fused_computation.10 | convolution fusion | flops 939851776 | bytes 268763648 | tf_op jit(solution)/shard_map/dot_general | solution.py:37
  172.5 0.2 copy.19
  172.7 1.8 broadcast_in_dim.2
  174.5 7.4 %all-to-all-start = ((bf16[128,2,2048]{0,1,2:T(2,128)(2,1)}), bf16[128,2,2048]{0,1,2:T(2,128)(2,1)S(1)}, u32[]{:S(2)}, u32[]{:S(2)}) async-start(bf16[128,2,2048]{0,1,2:T(2,128)(2,1)} %bitcast.8), calls=%async_computation | async-start | bytes 2097152 | tf_op jit(solution)/shard_map/all_to_all | solution.py:49
  181.9 21.7 %fusion = f32[128]{0:T(128)S(1)} fusion(bf16[128,268288]{1,0:T(8,128)(2,1)} %param.4), kind=kLoop, calls=%fused_computation.1 | loop fusion | flops 103022464 | bytes 68682240 | tf_op jit(solution)/shard_map/dot_general | solution.py:41
  203.7 21.9 %all-gather = f32[16,1,128]{2,1,0:T(1,128)S(1)} all-gather(f32[1,1,128]{2,1,0:T(1,128)S(1)} %add_bitcast_fusion), channel_id=1, replica_groups=mesh['group'=2,'inp'=16] {'inp'}, dimensions={0}, use_global_device_ids=true | all-gather | bytes 8704 | tf_op jit(solution)/shard_map/all_gather | solution.py:45
  225.6 0.1 dynamic-slice_multiply_fusion
  225.7 0.0 all-to-all-done
  225.7 0.1 copy.20
  225.8 0.7 copy.21
  226.5 0.7 copy.23
  227.2 2.7 %fusion.8 = f32[512,2048]{1,0:T(8,128)} fusion(bf16[2048,2,128]{2,0,1:T(8,128)(2,1)S(1)} %bitcast.49, s32[]{:T(128)S(6)} %select_n.19, s32[]{:T(128)S(6)} %add.38), kind=kOutput, calls=%fused_computation.15 | convolution fusion | flops 268435456 | bytes 4849672 | tf_op jit(solution)/shard_map/dot_general | solution.py:22
  229.9 0.1 copy.22
  230.1 2.9 %fusion.3 = bf16[512,1,2048]{2,0,1:T(8,128)(2,1)S(1)} fusion(f32[512,2048]{1,0:T(8,128)} %fusion.8, f32[2048]{0:T(1024)S(1)} %bitcast.55, f32[512]{0:T(512)S(1)} %dynamic-slice_multiply_fusion, bf16[2048,2,128]{2,0,1:T(8,128)(2,1)S(1)} %bitcast.50, s32[]{:T(128)S(6)} %select_n.19), kind=kOutput, calls=%fused_computation.8 | convolution fusion | flops 272629760 | bytes 6957060 | tf_op jit(solution)/shard_map/dot_general | solution.py:22
  233.0 0.8 fusion.2
  233.8 0.4 pad_maximum_fusion
  234.2 6.3 %copy.24 = bf16[512,2,2048]{2,1,0:T(2,128)(2,1)} copy(bf16[512,2,2048]{2,0,1:T(8,128)(2,1)S(1)} %pad_maximum_fusion) | data formatting | bytes 8388608 | tf_op jit(solution)/shard_map/stack | solution.py:65
  (5 shorter events, 0.1 us)
Async XLA Ops:
  0.0 88.5 %copy-start = (f32[4,2048]{1,0:T(4,128)S(1)}, f32[4,2048]{1,0:T(4,128)}, u32[]{:S(2)}) copy-start(f32[4,2048]{1,0:T(4,128)} %param.5) | copy-start | bytes 98308
  0.0 88.5 %copy-start.2 = (s32[128]{0:T(128)S(1)}, s32[128]{0:T(128)}, u32[]{:S(2)}) copy-start(s32[128]{0:T(128)} %param.6) | copy-start | bytes 1540
  0.0 88.5 %copy-start.1 = (s32[4]{0:T(128)S(1)}, s32[4]{0:T(128)}, u32[]{:S(2)}) copy-start(s32[4]{0:T(128)} %param.7) | copy-start | bytes 52
  174.5 51.2 %all-to-all-start = ((bf16[128,2,2048]{0,1,2:T(2,128)(2,1)}), bf16[128,2,2048]{0,1,2:T(2,128)(2,1)S(1)}, u32[]{:S(2)}, u32[]{:S(2)}) async-start(bf16[128,2,2048]{0,1,2:T(2,128)(2,1)} %bitcast.8), calls=%async_computation | async-start | bytes 2097152 | tf_op jit(solution)/shard_map/all_to_all | solution.py:49
where the time goes:
time: 243 us; the launch traced here: 240 us
  local copies, waits for them, and re-layouts  98.5 us (41%)
  matrix products  90 us (37%)
  other arithmetic  22.5 us (9%)
  blocking collectives  21.9 us (9%)
  starting transfers between devices  7.41 us (3%)
    unnamed x7, local copies, waits for them, and re-layouts  88.5 us
    dot_general x1, matrix products, on_device(): plain = jnp.dot(filtered, basis, preferred_element_type=jnp.float32)  83.6 us
    all_gather x1, blocking collectives, on_device(): power_all = lax.all_gather(power, 'inp', axis=0, tiled=True)  21.9 us
    dot_general x1, other arithmetic, on_device(): lax.dot_general(raw, raw, (((1,), (1,)), ((0,), (0,))), preferred_element...  21.7 us
    all_to_all x1, starting transfers between devices, on_device(): lax.all_to_all(outgoing, 'inp', split_axis=2, concat_axis=0, tiled=True)  7.41 us
    dot_general x3, matrix products, row_product(): lax.dot_general(left, right, (((1,), (1,)), ((), ())), preferred_element_...  6.4 us
    another operation x1, local copies, waits for them, and re-layouts, on_device(): return jnp.stack([real_out, imag_out], axis=1).astype(jnp.bfloat16)  6.33 us
  transfers between devices with their start and end apart: 1, of which 0 were waited for; matrix products, arithmetic and copies ran while one was open for 9% of the time, Pallas kernels for 0%

commit v1 on v0

--- a/solution.py
+++ b/solution.py
@@ -1,14 +1,21 @@
+import functools
 import math
 
 import jax
 import jax.numpy as jnp
 from jax import lax
+from jax.experimental import pallas as pl
+from jax.experimental.pallas import tpu as pltpu
 from jax.sharding import PartitionSpec as P
 
 FFT_LEN = 2048
 FILTER_TAPS = 4
 SPECTRA = 128
 ROW_BLOCKS = 4
+CHUNK = 8
+SLOTS = 3
+LANES = 128
+MESH = pl.DeviceIdType.MESH
 
 
 def make_basis(chan_table):
@@ -24,7 +31,7 @@
     )
 
 
-def on_device(raw, pfb_taps, flags, chan_table):
+def plain_device(raw, pfb_taps, flags, chan_table):
     width = raw.shape[0]
     count = SPECTRA
     frames = raw.reshape(width, count + FILTER_TAPS - 1, FFT_LEN)
@@ -65,10 +72,281 @@
     return jnp.stack([real_out, imag_out], axis=1).astype(jnp.bfloat16)
 
 
+def front_kernel(
+    n, raw, w_ref, flags_ref, g_out, p_out, buf, zbuf, abuf, cbuf, acc,
+    load_sem, s1, r1, s2, r2, sp, rp,
+):
+    width = flags_ref.shape[0]
+    lines = n // ROW_BLOCKS
+    group = lax.axis_index("group")
+    me = lax.axis_index("inp")
+    line, spot = me // ROW_BLOCKS, me % ROW_BLOCKS
+    full = SPECTRA // CHUNK
+    tail = FILTER_TAPS - 1
+
+    def load(c, slot, j):
+        return pltpu.make_async_copy(
+            raw.at[:, pl.ds((c * CHUNK + j) * FFT_LEN, FFT_LEN)],
+            buf.at[slot, pl.ds(j * width, width), :],
+            load_sem.at[slot, j],
+        )
+
+    def start(c, slot, frames):
+        for j in range(frames):
+            load(c, slot, j).start()
+
+    for c in range(SLOTS):
+        start(c, c, CHUNK)
+    barrier = pltpu.get_barrier_semaphore()
+    for step in range(1, n):
+        pl.semaphore_signal(
+            barrier, inc=1, device_id=(group, lax.rem(me + step, n)), device_id_type=MESH
+        )
+    acc[...] = jnp.zeros_like(acc)
+    zbuf[0 : tail * width, :] = jnp.zeros((tail * width, LANES), jnp.float32)
+    lane = lax.broadcasted_iota(jnp.int32, (width, LANES), 1)
+    pl.semaphore_wait(barrier, n - 1)
+
+    def process(slot, frames):
+        total = acc[...]
+        for j in range(frames):
+            for k in range(FFT_LEN // LANES):
+                x = buf[slot, j * width : (j + 1) * width, k * LANES : (k + 1) * LANES]
+                x = x.astype(jnp.float32)
+                total = total + x * x
+        acc[...] = total
+        y = jnp.dot(
+            buf[slot, 0 : frames * width, :], w_ref[...], preferred_element_type=jnp.float32
+        )
+        zbuf[tail * width : (tail + frames) * width, :] = y + pltpu.roll(y, LANES // 2, 1)
+        placed = jnp.zeros((width, LANES), jnp.float32)
+        for j in range(frames):
+            value = None
+            for p in range(FILTER_TAPS):
+                z = zbuf[(j + p) * width : (j + p + 1) * width, :]
+                shift = (j - p) * 8 % LANES
+                z = z if shift == 0 else pltpu.roll(z, shift, 1)
+                value = z if value is None else value + z
+            placed = jnp.where(lane // 8 == j, value, placed)
+        return placed
+
+    def first(g, step):
+        other = lax.rem(line + step, lines)
+        return pltpu.make_async_remote_copy(
+            src_ref=cbuf.at[other, g],
+            dst_ref=g_out.at[pl.ds(me * width, width), g * LANES : (g + 1) * LANES],
+            send_sem=s1.at[g, step - 1],
+            recv_sem=r1.at[g, step - 1],
+            device_id=(group, other * ROW_BLOCKS + spot),
+            device_id_type=MESH,
+        )
+
+    def second(g, step, turn):
+        source = lax.rem(line - step + lines, lines) * ROW_BLOCKS + spot
+        rows = g_out.at[pl.ds(source * width, width), g * LANES : (g + 1) * LANES]
+        return pltpu.make_async_remote_copy(
+            src_ref=cbuf.at[line, g] if step == 0 else rows,
+            dst_ref=rows,
+            send_sem=s2.at[g, step, turn - 1],
+            recv_sem=r2.at[g, step, turn - 1],
+            device_id=(group, line * ROW_BLOCKS + lax.rem(spot + turn, ROW_BLOCKS)),
+            device_id_type=MESH,
+        )
+
+    def send(g):
+        row = lax.broadcasted_iota(jnp.int32, (LANES, LANES), 0)
+        col = lax.broadcasted_iota(jnp.int32, (LANES, LANES), 1)
+        perm = jnp.where(
+            row == (col % 16) * 8 + (col // 16) % 2 * 4 + col // 32, 1.0, 0.0
+        ).astype(jnp.bfloat16)
+        flag = flags_ref[...]
+        columns = [jnp.zeros((width, LANES), jnp.float32)] * lines
+        for h in range(4):
+            d = (1 + 4 * g + h) % 8
+            both = jnp.where(
+                lane < LANES // 2, abuf[2 * d], pltpu.roll(abuf[2 * d + 1], LANES // 2, 1)
+            )
+            spectra = (both * flag).astype(jnp.bfloat16)
+            b = jnp.dot(spectra, perm, preferred_element_type=jnp.float32)
+            for k in range(lines):
+                shift = (h - k) * 32 % LANES
+                moved = b if shift == 0 else pltpu.roll(b, shift, 1)
+                columns[k] = jnp.where(lane // 32 == h, moved, columns[k])
+        for k in range(lines):
+            cbuf[k, g] = columns[k].astype(jnp.bfloat16)
+        for step in range(1, lines):
+            first(g, step).start()
+        for turn in range(1, ROW_BLOCKS):
+            second(g, 0, turn).start()
+        g_out[pl.ds(me * width, width), g * LANES : (g + 1) * LANES] = cbuf[line, g]
+
+    def forward(g):
+        for step in range(1, lines):
+            first(g, step).wait_recv()
+            for turn in range(1, ROW_BLOCKS):
+                second(g, step, turn).start()
+
+    def body(c, carry):
+        slot = lax.rem(c, SLOTS)
+        for j in range(CHUNK):
+            load(c, slot, j).wait()
+        abuf[c] = process(slot, CHUNK)
+
+        @pl.when(c + SLOTS < full)
+        def _():
+            start(c + SLOTS, slot, CHUNK)
+
+        @pl.when(c + SLOTS == full)
+        def _():
+            start(c + SLOTS, slot, tail)
+
+        zbuf[0 : tail * width, :] = zbuf[CHUNK * width : (CHUNK + tail) * width, :]
+
+        @pl.when(c == 9)
+        def _():
+            send(0)
+
+        @pl.when(c == 13)
+        def _():
+            forward(0)
+
+        return carry
+
+    lax.fori_loop(0, full, body, 0)
+    last = full % SLOTS
+    for j in range(tail):
+        load(full, last, j).wait()
+    placed = process(last, tail)
+    abuf[0] = jnp.where(lane < 8 * tail, placed, abuf[0])
+    send(1)
+    squares = jnp.sum(jnp.transpose(acc[...]), axis=0, keepdims=True)
+    power = squares * (1.0 / raw.shape[1]) + 1e-06
+    p_out[me] = jnp.broadcast_to(power, p_out.shape[1:])
+
+    def share(step):
+        return pltpu.make_async_remote_copy(
+            src_ref=p_out.at[me],
+            dst_ref=p_out.at[me],
+            send_sem=sp.at[step - 1],
+            recv_sem=rp.at[step - 1],
+            device_id=(group, lax.rem(me + step, n)),
+            device_id_type=MESH,
+        )
+
+    def shared(step):
+        source = lax.rem(me - step + n, n)
+        return pltpu.make_async_remote_copy(
+            src_ref=p_out.at[source],
+            dst_ref=p_out.at[source],
+            send_sem=sp.at[step - 1],
+            recv_sem=rp.at[step - 1],
+            device_id=(group, lax.rem(me + step, n)),
+            device_id_type=MESH,
+        )
+
+    def landed(g, step, turn):
+        source = lax.rem(line - step + lines, lines) * ROW_BLOCKS
+        source = source + lax.rem(spot - turn + ROW_BLOCKS, ROW_BLOCKS)
+        rows = g_out.at[pl.ds(source * width, width), g * LANES : (g + 1) * LANES]
+        return pltpu.make_async_remote_copy(
+            src_ref=rows,
+            dst_ref=rows,
+            send_sem=s2.at[g, step, turn - 1],
+            recv_sem=r2.at[g, step, turn - 1],
+            device_id=(group, line * ROW_BLOCKS + lax.rem(spot + turn, ROW_BLOCKS)),
+            device_id_type=MESH,
+        )
+
+    for step in range(1, n):
+        share(step).start()
+    forward(1)
+    for g in range(2):
+        for step in range(1, lines):
+            first(g, step).wait_send()
+        for step in range(lines):
+            for turn in range(1, ROW_BLOCKS):
+                second(g, step, turn).wait_send()
+                landed(g, step, turn).wait_recv()
+    for step in range(1, n):
+        share(step).wait_send()
+        shared(step).wait_recv()
+
+
+def make_weights(pfb_taps, chan_table):
+    basis = make_basis(chan_table).astype(jnp.float32)
+    product = pfb_taps.T[:, :, None] * basis[:, None, :]
+    product = product.reshape(FFT_LEN, -1)
+    high = lax.reduce_precision(product, 8, 7)
+    low = product - high
+    gap = LANES // 2 - product.shape[1]
+    padded = [jnp.pad(part, ((0, 0), (0, gap))) for part in (high, low)]
+    return jnp.concatenate(padded, axis=1).astype(jnp.bfloat16)
+
+
+def fast_device(n, raw, pfb_taps, flags, chan_table):
+    width = raw.shape[0]
+    lines = n // ROW_BLOCKS
+    weights = make_weights(pfb_taps, chan_table)
+    vmem = pl.BlockSpec(memory_space=pltpu.VMEM)
+    full = SPECTRA // CHUNK
+    rows = CHUNK * width
+    columns, power_all = pl.pallas_call(
+        functools.partial(front_kernel, n),
+        out_shape=(
+            jax.ShapeDtypeStruct((n * width, 2 * LANES), jnp.bfloat16),
+            jax.ShapeDtypeStruct((n, 8, LANES), jnp.float32),
+        ),
+        in_specs=[pl.BlockSpec(memory_space=pl.ANY), vmem, vmem],
+        out_specs=(vmem, vmem),
+        scratch_shapes=[
+            pltpu.VMEM((SLOTS, rows, FFT_LEN), jnp.bfloat16),
+            pltpu.VMEM((rows + (FILTER_TAPS - 1) * width, LANES), jnp.float32),
+            pltpu.VMEM((full, width, LANES), jnp.float32),
+            pltpu.VMEM((lines, 2, width, LANES), jnp.bfloat16),
+            pltpu.VMEM((width, LANES), jnp.float32),
+            pltpu.SemaphoreType.DMA((SLOTS, CHUNK)),
+            pltpu.SemaphoreType.DMA((2, lines - 1)),
+            pltpu.SemaphoreType.DMA((2, lines - 1)),
+            pltpu.SemaphoreType.DMA((2, lines, ROW_BLOCKS - 1)),
+            pltpu.SemaphoreType.DMA((2, lines, ROW_BLOCKS - 1)),
+            pltpu.SemaphoreType.DMA((n - 1,)),
+            pltpu.SemaphoreType.DMA((n - 1,)),
+        ],
+        compiler_params=pltpu.CompilerParams(collective_id=0, has_side_effects=True),
+    )(raw, weights, flags.astype(jnp.float32)[:, None])
+    return finish(columns, power_all[:, 0, :].reshape(-1))
+
+
+def finish(columns, power_all):
+    total = columns.shape[0]
+    rows_here = total // ROW_BLOCKS
+    start = lax.axis_index("inp") % ROW_BLOCKS * rows_here
+    mine = lax.dynamic_slice_in_dim(columns, start, rows_here, 0)
+    halves = mine.reshape(rows_here, 8, 2, 16)
+    turned = jnp.stack([halves[:, :, 1], -halves[:, :, 0]], axis=2)
+    turned = turned.reshape(rows_here, 2 * LANES)
+    real_vis = row_product(mine, columns)
+    imag_vis = row_product(turned, columns)
+    scales = lax.rsqrt(power_all)
+    my_scales = lax.dynamic_slice_in_dim(scales, start, rows_here, 0)
+    left_scale = my_scales[:, None] * (1.0 / SPECTRA)
+    right_scale = scales[None, :]
+    real_out = real_vis * left_scale * right_scale
+    imag_out = imag_vis * left_scale * right_scale
+    return jnp.stack([real_out, imag_out], axis=1).astype(jnp.bfloat16)
+
+
+def on_device(n, raw, pfb_taps, flags, chan_table):
+    fits = n == ROW_BLOCKS * chan_table.shape[0] and chan_table.shape[0] == 4
+    if fits and raw.shape[0] == LANES:
+        return fast_device(n, raw, pfb_taps, flags, chan_table)
+    return plain_device(raw, pfb_taps, flags, chan_table)
+
+
 def solution(mesh):
     placed = (P(("group", "inp"), None), P(), P(("group", "inp")), P("group"))
     return jax.shard_map(
-        on_device,
+        functools.partial(on_device, mesh.shape["inp"]),
         mesh=mesh,
         in_specs=placed,
         out_specs=P(("group", "inp"), None, None),

time: 243 us -> 75.5 us (0.31)
  local copies, waits for them, and re-layouts: 98.5 us -> 9.78 us
  matrix products: 90 us -> 2.97 us
  Pallas kernels: 0 us -> 57.2 us
  blocking collectives: 21.9 us -> 0 us
  other arithmetic: 22.5 us -> 5.05 us
  starting transfers between devices: 7.41 us -> 0 us
    unnamed x7 -> x2, local copies, waits for them, and re-layouts: 88.5 us -> 0.01 us
    dot_general x1 -> x0, matrix products: 83.6 us -> none  [on_device(): plain = jnp.dot(filtered, basis, preferred_element_type=jnp.float32)]
    pallas_call x0 -> x1, Pallas kernels: none -> 57.2 us  [fast_device(): pl.pallas_call(functools.partial(front_kernel, n), out_shape=(jax.ShapeDt...]
    all_gather x1 -> x0, blocking collectives: 21.9 us -> none  [on_device(): power_all = lax.all_gather(power, 'inp', axis=0, tiled=True)]
    dot_general x1 -> x0, other arithmetic: 21.7 us -> none  [on_device(): lax.dot_general(raw, raw, (((1,), (1,)), ((0,), (0,))), preferred_element...]
    all_to_all x1 -> x0, starting transfers between devices: 7.41 us -> none  [on_device(): lax.all_to_all(outgoing, 'inp', split_axis=2, concat_axis=0, tiled=True)]
    dot_general x3 -> x2, matrix products: 6.4 us -> 2.97 us  [row_product(): lax.dot_general(left, right, (((1,), (1,)), ((), ())), preferred_element_...]
  transfers between devices with their start and end apart: 1 -> 0, of which waited for: 0 -> 0; matrix products, arithmetic and copies ran while one was open for 9% -> 0% of each run, Pallas kernels for 0% -> 0%
where the time goes in v1:
time: 75.5 us; the launch traced here: 75.1 us
  Pallas kernels  57.2 us (76%)
  local copies, waits for them, and re-layouts  9.78 us (13%)
  other arithmetic  5.05 us (7%)
  matrix products  2.97 us (4%)
    pallas_call x1, Pallas kernels, fast_device(): pl.pallas_call(functools.partial(front_kernel, n), out_shape=(jax.ShapeDt...  57.2 us
    another operation x1, local copies, waits for them, and re-layouts, finish(): return jnp.stack([real_out, imag_out], axis=1).astype(jnp.bfloat16)  6.33 us
    dot_general x2, matrix products, row_product(): lax.dot_general(left, right, (((1,), (1,)), ((), ())), preferred_element_...  2.97 us

profile of v1, /device:TPU:0, one launch (start us, length us, event | category | flops | bytes accessed | tf_op | source)
XLA Modules:
  0.0 75.1 jit_solution(16783968861109128205)
XLA Ops:
  0.0 0.7 convert_bitcast_fusion
  0.7 1.0 %cosine_convert_fusion = (bf16[2048,4]{0,1:T(4,128)(2,1)S(1)}, bf16[2048,4]{0,1:T(4,128)(2,1)S(1)}) fusion(s32[4]{0:T(128)} %param.7), kind=kLoop, calls=%fused_computation.23 | loop fusion | flops 139264 | bytes 32784 | tf_op jit(solution)/shard_map/convert.10
  1.7 0.7 copy.16.flags_ref
  2.4 0.8 %fusion.5 = f32[2048,32]{0,1:T(8,128)S(1)} fusion(f32[2048,8]{0,1:T(8,128)S(1)} %maximum_convert_fusion, f32[2048,4]{0,1:T(4,128)} %bitcast.20), kind=kLoop, calls=%fused_computation.14 | loop fusion | flops 131072 | bytes 360448 | tf_op jit(solution)/shard_map/reduce_precision | solution.py:279
  3.2 0.8 %multiply_bitcast_fusion = f32[2048,32]{0,1:T(8,128)S(1)} fusion(f32[2048,8]{0,1:T(8,128)S(1)} %maximum_convert_fusion, f32[2048,4]{0,1:T(4,128)} %bitcast.21), kind=kLoop, calls=%fused_computation.12 | loop fusion | flops 65536 | bytes 360448 | tf_op jit(solution)/shard_map/mul | solution.py:277
  4.0 0.3 copy.14
  4.3 0.3 copy.13
  4.7 0.1 fusion.9
  4.8 1.2 %fusion.4.w_ref = bf16[2048,128]{1,0:T(8,128)(2,1)} fusion(bf16[2048,32]{1,0:T(8,128)(2,1)S(1)} %get-tuple-element.10, bf16[2048,32]{1,0:T(8,128)(2,1)S(1)} %get-tuple-element.9), kind=kLoop, calls=%fused_computation.10 | loop fusion | flops 2097152 | bytes 786432 | tf_op jit(solution)/shard_map/concatenate | solution.py:283
  6.0 57.2 %shard_map.46 = (bf16[2048,256]{1,0:T(8,128)(2,1)}, f32[16,8,128]{2,1,0:T(8,128)}) custom-call(bf16[128,268288]{1,0:T(8,128)(2,1)} %raw.1, bf16[2048,128]{1,0:T(8,128)(2,1)} %fusion.4.w_ref, f32[128,1]{1,0:T(8,128)} %copy.16.flags_ref), custom_call_target="tpu_custom_call" | custom-call | tf_op jit(solution)/shard_map/pallas_call | solution.py:293
  63.2 0.0 copy-start
  63.2 0.9 %slice_rsqrt_fusion = f32[16,1,128]{2,1,0:T(1,128)S(1)} fusion(f32[16,8,128]{2,1,0:T(8,128)} %get-tuple-element.8), kind=kLoop, calls=%fused_computation.24 | loop fusion | bytes 16384 | tf_op jit(solution)/shard_map/rsqrt | solution.py:330
  64.1 0.1 dynamic-slice_multiply_fusion
  64.2 1.0 %constant_dynamic-slice_fusion = bf16[512,256]{1,0:T(8,128)(2,1)S(1)} fusion(bf16[2048,256]{1,0:T(8,128)(2,1)} %get-tuple-element.7, s32[]{:T(128)S(6)} %select_n.23), kind=kLoop, calls=%fused_computation.27 | loop fusion | bytes 524292 | tf_op jit(solution)/shard_map/dynamic_slice | solution.py:324
  65.2 0.1 copy.17
  65.4 2.2 %fusion.1 = bf16[512,1,2048]{2,0,1:T(8,128)(2,1)S(1)} fusion(bf16[512,256]{0,1:T(8,128)(2,1)S(1)} %bitcast.19, bf16[2048,256]{1,0:T(8,128)(2,1)} %get-tuple-element.7, f32[2048]{0:T(1024)S(1)} %bitcast.23, f32[512]{0:T(512)S(1)} %dynamic-slice_multiply_fusion), kind=kOutput, calls=%fused_computation.4 | convolution fusion | flops 540016640 | bytes 3418112 | tf_op jit(solution)/shard_map/dot_general | solution.py:29
  67.6 0.0 copy-done
  67.6 0.7 fusion
  68.4 0.4 pad_maximum_fusion
  68.8 6.3 %copy.18 = bf16[512,2,2048]{2,1,0:T(2,128)(2,1)} copy(bf16[512,2,2048]{2,0,1:T(8,128)(2,1)S(1)} %pad_maximum_fusion) | data formatting | bytes 8388608 | tf_op jit(solution)/shard_map/stack | solution.py:336
  (3 shorter events, 0.1 us)
Async XLA Ops:
  63.2 4.5 %copy-start = (bf16[2048,256]{1,0:T(8,128)(2,1)S(1)}, bf16[2048,256]{1,0:T(8,128)(2,1)}, u32[]{:S(2)}) copy-start(bf16[2048,256]{1,0:T(8,128)(2,1)} %get-tuple-element.7) | copy-start | bytes 3145732
